TPU v7x, 512 devices: a whole 4x8x8 slice. The times are simulated.
512 devices in a mesh: band: 32 (over z_lo, y, core), dom: 16 (over z_hi, x).
Axes of the slice: x: 4, y: 8, z: 8 (z_hi: 4, z_lo: 2; z = z_hi * 2 + z_lo), core: 2. Of those that a mesh axis runs over, the one named last changes fastest.
Arguments:
- states: float32 [4096, 8, 128, 128], P('band', None, 'dom'), may hold values from -0.015625 to 0.015625
- window: float32 [128, 8, 128, 128], P('band', None, 'dom'), may hold values from -6 to 6
- potential: float32 [8, 128, 128], P(None, 'dom'), may hold values from -3 to 3
Outputs:
- intersection: float32 [4096, 128], P('band')
- hamiltonian: float32 [4096, 128], P('band')
All inputs are finite; a program needn't handle non-finite values.
Results may differ from a plain program's by a relative error of at most 0.00012.
Values sent between devices are 32-bit elements; how exact they have to be, the bound alone decides.
A program may use at most 64 MiB of HBM per device.

v0:
```python
import jax
import jax.numpy as jnp
from jax import lax
from jax.sharding import PartitionSpec as P

DEGREE = 4
coeffs = (
    -5369.0 / 1800.0,
    12.0 / 7.0,
    -15.0 / 56.0,
    10.0 / 189.0,
    -1.0 / 112.0,
    2.0 / 1925.0,
    -1.0 / 16632.0,
)
centre_value = 9.0
half_width = 7.0


def padded(block, sides, width):
    for axis, dim in sides:
        count = lax.axis_size(axis)
        forward = [(i, i + 1) for i in range(count - 1)]
        forward.append((count - 1, 0))
        backward = [(target, source) for source, target in forward]
        low = lax.ppermute(
            lax.slice_in_dim(block, block.shape[dim] - width, None, axis=dim), axis, forward
        )
        high = lax.ppermute(lax.slice_in_dim(block, 0, width, axis=dim), axis, backward)
        block = jnp.concatenate([low, block, high], axis=dim)
    return block


def stencil_sum(wave_in, padded_x, padded_y, potential):
    x_cells = wave_in.shape[2]
    y_cells = wave_in.shape[3]
    z_cells = wave_in.shape[1]
    along_z = jnp.pad(wave_in, ((0, 0), (6, 6), (0, 0), (0, 0)))
    laplace = 3.0 * coeffs[0] * wave_in
    for offset in range(1, 7):
        beside = (
            padded_x[:, :, 6 + offset : 6 + offset + x_cells]
            + padded_x[:, :, 6 - offset : 6 - offset + x_cells]
        )
        beside = (
            beside
            + padded_y[:, :, :, 6 + offset : 6 + offset + y_cells]
            + padded_y[:, :, :, 6 - offset : 6 - offset + y_cells]
        )
        beside = (
            beside
            + along_z[:, 6 + offset : 6 + offset + z_cells]
            + along_z[:, 6 - offset : 6 - offset + z_cells]
        )
        laplace = laplace + coeffs[offset] * beside
    return -0.5 * laplace + potential * wave_in


def apply_banded(wave_in, potential):
    padded_x = padded(wave_in, (("dom", 2),), 6)
    padded_y = jnp.concatenate((wave_in[:, :, :, -6:], wave_in, wave_in[:, :, :, :6]), axis=3)
    return stencil_sum(wave_in, padded_x, padded_y, potential)


def chebyshev(window, operate):
    previous = window
    current = (operate(window) - centre_value * window) / half_width
    for repeat_index in range(DEGREE - 1):
        following = 2.0 * (operate(current) - centre_value * current) / half_width - previous
        previous, current = (current, following)
    image = operate(current)
    return jnp.stack((current, image))


def per_device(states, window, potential):
    stacked = chebyshev(window, lambda wave: apply_banded(wave, potential))
    states_flat = states.reshape(states.shape[0], -1)
    whole_window = lax.all_gather(stacked, "band", axis=1, tiled=True)
    flat_piece = whole_window.reshape(-1, states_flat.shape[1])
    product = lax.dot_general(
        states_flat,
        flat_piece,
        (((1,), (1,)), ((), ())),
        precision=lax.Precision.HIGHEST,
        preferred_element_type=jnp.float32,
    )
    partial_value = product.reshape(states_flat.shape[0], 2, whole_window.shape[1])
    totals = lax.psum(partial_value, "dom")
    return (totals[:, 0, :], totals[:, 1, :])


def solution(mesh):
    in_specs = (P("band", None, "dom", None), P("band", None, "dom", None), P(None, "dom", None))
    out_specs = (P("band", None), P("band", None))
    return jax.shard_map(
        per_device, mesh=mesh, in_specs=in_specs, out_specs=out_specs, check_vma=False
    )
```

profile of v0, /device:TPU:8, one launch (start us, length us, event | category | flops | bytes accessed | tf_op | source)
XLA Modules:
  0.0 371.7 jit_solution(3588212571015930287)
XLA Ops:
  7.2 0.0 copy-start
  7.2 0.0 all-gather.2.cloned.1.call-start
  7.2 1.0 fusion.338
  8.2 13.1 %collective-permute-start = (f32[4,8,6,128]{3,2,1,0:T(8,128)S(1)}, f32[4,8,6,128]{3,2,1,0:T(8,128)S(1)}, u32[]{:S(2)}, u32[]{:S(2)}) collective-permute-start(f32[4,8,6,128]{3,2,1,0:T(8,128)S(1)} %get-tuple-element.22), channel_id=1, source_target_pairs={{1,0},{2,1},{3,2},{4,3},{5,4},{6,5},{7,6},{8,7},{9,8},{10,9},{11,1... | collective-permute-start | bytes 294920 | tf_op jit(solution)/shard_map/ppermute | solution.py:29
  21.4 1.9 collective-permute-start.1
  23.3 1.1 fusion.339
  24.4 0.8 broadcast_multiply_fusion.1
  25.1 0.9 constant_dynamic-update-slice_fusion.1
  26.1 0.8 collective-permute-done
  26.9 7.5 %collective-permute-done.1 = f32[4,8,6,128]{3,2,1,0:T(8,128)S(1)} collective-permute-done((f32[4,8,6,128]{3,2,1,0:T(8,128)S(1)}, f32[4,8,6,128]{3,2,1,0:T(8,128)S(1)}, u32[]{:S(2)}, u32[]{:S(2)}) %collective-permute-start.1) | collective-permute-done | bytes 98336 | tf_op jit(solution)/shard_map/ppermute | solution.py:26
  34.5 5.2 %broadcast_multiply_fusion = (f32[4,8,8,128]{3,2,1,0:T(8,128)S(1)}, f32[4,8,8,128]{3,2,1,0:T(8,128)S(1)}) fusion(f32[4,8,8,128]{3,2,1,0:T(8,128)} %param.4, f32[8,8,128]{2,1,0:T(8,128)} %param.5, f32[4,8,8,6]{3,2,1,0:T(8,128)S(1)} %get-tuple-element.25, f32[4,8,8,6]{3,2,1,0:T(8,128)S(1)} %get-tuple-element.24, ...), kind=kLoop, calls=%fused_computation.601 | loop fusion | flops 2195456 | bytes 1323008 | tf_op jit(solution)/shard_map/div | solution.py:67
  39.7 1.9 collective-permute-start.2
  41.6 3.9 %collective-permute-start.3 = (f32[4,8,6,128]{3,2,1,0:T(8,128)S(1)}, f32[4,8,6,128]{3,2,1,0:T(8,128)S(1)}, u32[]{:S(2)}, u32[]{:S(2)}) collective-permute-start(f32[4,8,6,128]{3,2,1,0:T(8,128)S(1)} %get-tuple-element.19), channel_id=1, source_target_pairs={{0,1},{1,2},{2,3},{3,4},{4,5},{5,6},{6,7},{7,8},{8,9},{9,10},{10,1... | collective-permute-start | bytes 294920 | tf_op jit(solution)/shard_map/ppermute | solution.py:26
  45.6 0.1 fusion.337
  45.7 1.8 collective-permute-done.2
  47.5 7.0 %collective-permute-done.3 = f32[4,8,6,128]{3,2,1,0:T(8,128)S(1)} collective-permute-done((f32[4,8,6,128]{3,2,1,0:T(8,128)S(1)}, f32[4,8,6,128]{3,2,1,0:T(8,128)S(1)}, u32[]{:S(2)}, u32[]{:S(2)}) %collective-permute-start.3) | collective-permute-done | bytes 98336 | tf_op jit(solution)/shard_map/ppermute | solution.py:26
  54.5 1.8 fusion.195
  56.2 1.9 collective-permute-start.4
  58.2 3.9 %collective-permute-start.5 = (f32[4,8,6,128]{3,2,1,0:T(8,128)S(1)}, f32[4,8,6,128]{3,2,1,0:T(8,128)S(1)}, u32[]{:S(2)}, u32[]{:S(2)}) collective-permute-start(f32[4,8,6,128]{3,2,1,0:T(8,128)S(1)} %get-tuple-element.15), channel_id=1, source_target_pairs={{0,1},{1,2},{2,3},{3,4},{4,5},{5,6},{6,7},{7,8},{8,9},{9,10},{10,1... | collective-permute-start | bytes 294920 | tf_op jit(solution)/shard_map/ppermute | solution.py:26
  62.1 0.1 fusion.335
  62.2 0.9 collective-permute-done.4
  63.1 6.2 %collective-permute-done.5 = f32[4,8,6,128]{3,2,1,0:T(8,128)S(1)} collective-permute-done((f32[4,8,6,128]{3,2,1,0:T(8,128)S(1)}, f32[4,8,6,128]{3,2,1,0:T(8,128)S(1)}, u32[]{:S(2)}, u32[]{:S(2)}) %collective-permute-start.5) | collective-permute-done | bytes 98336 | tf_op jit(solution)/shard_map/ppermute | solution.py:26
  69.3 1.6 fusion.134
  70.9 1.9 collective-permute-start.6
  72.9 3.9 %collective-permute-start.7 = (f32[4,8,6,128]{3,2,1,0:T(8,128)S(1)}, f32[4,8,6,128]{3,2,1,0:T(8,128)S(1)}, u32[]{:S(2)}, u32[]{:S(2)}) collective-permute-start(f32[4,8,6,128]{3,2,1,0:T(8,128)S(1)} %get-tuple-element.11), channel_id=1, source_target_pairs={{0,1},{1,2},{2,3},{3,4},{4,5},{5,6},{6,7},{7,8},{8,9},{9,10},{10,1... | collective-permute-start | bytes 294920 | tf_op jit(solution)/shard_map/ppermute | solution.py:26
  76.8 0.1 fusion.333
  76.9 0.9 collective-permute-done.6
  77.8 6.8 %collective-permute-done.7 = f32[4,8,6,128]{3,2,1,0:T(8,128)S(1)} collective-permute-done((f32[4,8,6,128]{3,2,1,0:T(8,128)S(1)}, f32[4,8,6,128]{3,2,1,0:T(8,128)S(1)}, u32[]{:S(2)}, u32[]{:S(2)}) %collective-permute-start.7) | collective-permute-done | bytes 98336 | tf_op jit(solution)/shard_map/ppermute | solution.py:26
  84.6 0.0 copy-done
  84.6 0.9 fusion.73
  85.5 1.9 collective-permute-start.8
  87.4 3.9 %collective-permute-start.9 = (f32[4,8,6,128]{3,2,1,0:T(8,128)S(1)}, f32[4,8,6,128]{3,2,1,0:T(8,128)S(1)}, u32[]{:S(2)}, u32[]{:S(2)}) collective-permute-start(f32[4,8,6,128]{3,2,1,0:T(8,128)S(1)} %get-tuple-element.7), channel_id=1, source_target_pairs={{0,1},{1,2},{2,3},{3,4},{4,5},{5,6},{6,7},{7,8},{8,9},{9,10},{10,1... | collective-permute-start | bytes 294920 | tf_op jit(solution)/shard_map/ppermute | solution.py:26
  91.3 0.1 fusion.331
  91.4 0.9 collective-permute-done.8
  92.3 6.1 %collective-permute-done.9 = f32[4,8,6,128]{3,2,1,0:T(8,128)S(1)} collective-permute-done((f32[4,8,6,128]{3,2,1,0:T(8,128)S(1)}, f32[4,8,6,128]{3,2,1,0:T(8,128)S(1)}, u32[]{:S(2)}, u32[]{:S(2)}) %collective-permute-start.9) | collective-permute-done | bytes 98336 | tf_op jit(solution)/shard_map/ppermute | solution.py:26
  98.5 0.9 fusion.12
  99.3 0.7 pad_maximum_fusion
  100.1 0.0 all-gather.2.cloned.1.call-update
  100.1 0.0 all-reduce.7.cloned.1.call-start
  100.1 69.7 %all-gather.2.cloned.1.call-done = f32[2,128,8,8,128]{4,3,2,1,0:T(8,128)} async-done(((f32[2,4,8,8,128]{4,3,2,1,0:T(8,128)}), f32[2,128,8,8,128]{4,3,2,1,0:T(8,128)}) %all-gather.2.cloned.1.call-update) | async-done | bytes 8388624 | tf_op jit(solution)/shard_map/all_gather | solution.py:78
  169.9 9.4 %reshape.14 = f32[256,8192]{1,0:T(8,128)} reshape(f32[2,128,8,8,128]{4,3,2,1,0:T(8,128)} %all-gather.2.cloned.1.call-done) | data formatting | bytes 16777216 | tf_op jit(solution)/shard_map/reshape | solution.py:79
  179.2 11.7 %fusion = f32[256,128]{1,0:T(8,128)S(1)} fusion(f32[256,8192]{1,0:T(8,128)} %reshape.14, f32[16,8,64,128]{3,2,1,0:T(8,128)} %bitcast.19), kind=kOutput, calls=%fused_computation | convolution fusion | flops 3221225472 | bytes 12713984 | tf_op jit(solution)/shard_map/dot_general | solution.py:80
  191.0 0.7 copy.5
  191.7 0.0 all-reduce.7.cloned.1.call-update
  191.7 171.6 %all-reduce.7.cloned.1.call-done = f32[128,2,128]{2,0,1:T(8,128)} async-done(((f32[128,2,128]{2,0,1:T(8,128)}), f32[128,2,128]{2,0,1:T(8,128)}) %all-reduce.7.cloned.1.call-update) | async-done | bytes 131088 | tf_op jit(solution)/shard_map/psum | solution.py:88
  363.4 1.5 slice_bitcast_fusion
  (5 shorter events, 0.1 us)
Async XLA Ops:
  7.2 77.4 %copy-start = (f32[8,8,128]{2,1,0:T(8,128)S(1)}, f32[8,8,128]{2,1,0:T(8,128)}, u32[]{:S(2)}) copy-start(f32[8,8,128]{2,1,0:T(8,128)} %param.5) | copy-start | bytes 98308
  7.2 162.7 %all-gather.2.cloned.1.call-start = ((), (), s32[]{:S(2)}) async-start(), calls=%async_computation | async-start | bytes 8650752 | tf_op jit(solution)/shard_map/all_gather | solution.py:78
  8.2 18.7 %collective-permute-start = (f32[4,8,6,128]{3,2,1,0:T(8,128)S(1)}, f32[4,8,6,128]{3,2,1,0:T(8,128)S(1)}, u32[]{:S(2)}, u32[]{:S(2)}) collective-permute-start(f32[4,8,6,128]{3,2,1,0:T(8,128)S(1)} %get-tuple-element.22), channel_id=1, source_target_pairs={{1,0},{2,1},{3,2},{4,3},{5,4},{6,5},{7,6},{8,7},{9,8},{10,9},{11,1... | collective-permute-start | bytes 294920 | tf_op jit(solution)/shard_map/ppermute | solution.py:29
  21.4 13.1 %collective-permute-start.1 = (f32[4,8,6,128]{3,2,1,0:T(8,128)S(1)}, f32[4,8,6,128]{3,2,1,0:T(8,128)S(1)}, u32[]{:S(2)}, u32[]{:S(2)}) collective-permute-start(f32[4,8,6,128]{3,2,1,0:T(8,128)S(1)} %get-tuple-element.23), channel_id=1, source_target_pairs={{0,1},{1,2},{2,3},{3,4},{4,5},{5,6},{6,7},{7,8},{8,9},{9,10},{10,1... | collective-permute-start | bytes 294920 | tf_op jit(solution)/shard_map/ppermute | solution.py:26
  39.7 7.8 %collective-permute-start.2 = (f32[4,8,6,128]{3,2,1,0:T(8,128)S(1)}, f32[4,8,6,128]{3,2,1,0:T(8,128)S(1)}, u32[]{:S(2)}, u32[]{:S(2)}) collective-permute-start(f32[4,8,6,128]{3,2,1,0:T(8,128)S(1)} %get-tuple-element.18), channel_id=1, source_target_pairs={{1,0},{2,1},{3,2},{4,3},{5,4},{6,5},{7,6},{8,7},{9,8},{10,9},{11,1... | collective-permute-start | bytes 294920 | tf_op jit(solution)/shard_map/ppermute | solution.py:29
  41.6 12.8 %collective-permute-start.3 = (f32[4,8,6,128]{3,2,1,0:T(8,128)S(1)}, f32[4,8,6,128]{3,2,1,0:T(8,128)S(1)}, u32[]{:S(2)}, u32[]{:S(2)}) collective-permute-start(f32[4,8,6,128]{3,2,1,0:T(8,128)S(1)} %get-tuple-element.19), channel_id=1, source_target_pairs={{0,1},{1,2},{2,3},{3,4},{4,5},{5,6},{6,7},{7,8},{8,9},{9,10},{10,1... | collective-permute-start | bytes 294920 | tf_op jit(solution)/shard_map/ppermute | solution.py:26
  56.2 6.9 %collective-permute-start.4 = (f32[4,8,6,128]{3,2,1,0:T(8,128)S(1)}, f32[4,8,6,128]{3,2,1,0:T(8,128)S(1)}, u32[]{:S(2)}, u32[]{:S(2)}) collective-permute-start(f32[4,8,6,128]{3,2,1,0:T(8,128)S(1)} %get-tuple-element.14), channel_id=1, source_target_pairs={{1,0},{2,1},{3,2},{4,3},{5,4},{6,5},{7,6},{8,7},{9,8},{10,9},{11,1... | collective-permute-start | bytes 294920 | tf_op jit(solution)/shard_map/ppermute | solution.py:29
  58.2 11.1 %collective-permute-start.5 = (f32[4,8,6,128]{3,2,1,0:T(8,128)S(1)}, f32[4,8,6,128]{3,2,1,0:T(8,128)S(1)}, u32[]{:S(2)}, u32[]{:S(2)}) collective-permute-start(f32[4,8,6,128]{3,2,1,0:T(8,128)S(1)} %get-tuple-element.15), channel_id=1, source_target_pairs={{0,1},{1,2},{2,3},{3,4},{4,5},{5,6},{6,7},{7,8},{8,9},{9,10},{10,1... | collective-permute-start | bytes 294920 | tf_op jit(solution)/shard_map/ppermute | solution.py:26
  70.9 6.9 %collective-permute-start.6 = (f32[4,8,6,128]{3,2,1,0:T(8,128)S(1)}, f32[4,8,6,128]{3,2,1,0:T(8,128)S(1)}, u32[]{:S(2)}, u32[]{:S(2)}) collective-permute-start(f32[4,8,6,128]{3,2,1,0:T(8,128)S(1)} %get-tuple-element.10), channel_id=1, source_target_pairs={{1,0},{2,1},{3,2},{4,3},{5,4},{6,5},{7,6},{8,7},{9,8},{10,9},{11,1... | collective-permute-start | bytes 294920 | tf_op jit(solution)/shard_map/ppermute | solution.py:29
  72.9 11.7 %collective-permute-start.7 = (f32[4,8,6,128]{3,2,1,0:T(8,128)S(1)}, f32[4,8,6,128]{3,2,1,0:T(8,128)S(1)}, u32[]{:S(2)}, u32[]{:S(2)}) collective-permute-start(f32[4,8,6,128]{3,2,1,0:T(8,128)S(1)} %get-tuple-element.11), channel_id=1, source_target_pairs={{0,1},{1,2},{2,3},{3,4},{4,5},{5,6},{6,7},{7,8},{8,9},{9,10},{10,1... | collective-permute-start | bytes 294920 | tf_op jit(solution)/shard_map/ppermute | solution.py:26
  85.5 6.9 %collective-permute-start.8 = (f32[4,8,6,128]{3,2,1,0:T(8,128)S(1)}, f32[4,8,6,128]{3,2,1,0:T(8,128)S(1)}, u32[]{:S(2)}, u32[]{:S(2)}) collective-permute-start(f32[4,8,6,128]{3,2,1,0:T(8,128)S(1)} %get-tuple-element.6), channel_id=1, source_target_pairs={{1,0},{2,1},{3,2},{4,3},{5,4},{6,5},{7,6},{8,7},{9,8},{10,9},{11,1... | collective-permute-start | bytes 294920 | tf_op jit(solution)/shard_map/ppermute | solution.py:29
  87.4 11.1 %collective-permute-start.9 = (f32[4,8,6,128]{3,2,1,0:T(8,128)S(1)}, f32[4,8,6,128]{3,2,1,0:T(8,128)S(1)}, u32[]{:S(2)}, u32[]{:S(2)}) collective-permute-start(f32[4,8,6,128]{3,2,1,0:T(8,128)S(1)} %get-tuple-element.7), channel_id=1, source_target_pairs={{0,1},{1,2},{2,3},{3,4},{4,5},{5,6},{6,7},{7,8},{8,9},{9,10},{10,1... | collective-permute-start | bytes 294920 | tf_op jit(solution)/shard_map/ppermute | solution.py:26
  100.1 263.3 %all-reduce.7.cloned.1.call-start = ((), (), s32[]{:S(2)}) async-start(), calls=%async_computation.1 | async-start | bytes 262144 | tf_op jit(solution)/shard_map/psum | solution.py:88
Sparse Core Ops, SparseCore 0:
  100.2 69.6 all-gather.1
  191.9 171.4 all-reduce.6
where the time goes:
time: 373 us; the launch traced here: 372 us
  waiting for transfers between devices  280 us (75%)
  starting transfers between devices  38.5 us (10%)
  local copies, waits for them, and re-layouts  15.1 us (4%)
  between operations  14.2 us (4%)
  other arithmetic  11.8 us (3%)
  matrix products  11.7 us (3%)
    psum x1, waiting for transfers between devices, per_device(): totals = lax.psum(partial_value, 'dom')  172 us
    all_gather x1, waiting for transfers between devices, per_device(): whole_window = lax.all_gather(stacked, 'band', axis=1, tiled=True)  69.7 us
    ppermute x5, waiting for transfers between devices, padded(): lax.ppermute(lax.slice_in_dim(block, block.shape[dim] - width, None, axis...  33.6 us
    ppermute x5, starting transfers between devices, padded(): lax.ppermute(lax.slice_in_dim(block, 0, width, axis=dim), axis, backward)  20.8 us
    ppermute x5, starting transfers between devices, padded(): lax.ppermute(lax.slice_in_dim(block, block.shape[dim] - width, None, axis...  17.6 us
    dot_general x1, matrix products, per_device(): lax.dot_general(states_flat, flat_piece, (((1,), (1,)), ((), ())), precis...  11.7 us
    reshape x1, local copies, waits for them, and re-layouts, per_device(): flat_piece = whole_window.reshape(-1, states_flat.shape[1])  9.36 us
  transfers between devices with their start and end apart: 12, of which 12 were waited for; matrix products, arithmetic and copies ran while one was open for 1% of the time, Pallas kernels for 0%

commit v1 on v0

--- a/solution.py
+++ b/solution.py
@@ -15,6 +15,12 @@
 )
 centre_value = 9.0
 half_width = 7.0
+
+
+def gather_and_add(value, axis):
+    parts = lax.all_gather(value, axis, axis=0, tiled=False)
+    result = parts.sum(axis=0)
+    return result
 
 
 def padded(block, sides, width):
@@ -85,7 +91,7 @@
         preferred_element_type=jnp.float32,
     )
     partial_value = product.reshape(states_flat.shape[0], 2, whole_window.shape[1])
-    totals = lax.psum(partial_value, "dom")
+    totals = gather_and_add(partial_value, "dom")
     return (totals[:, 0, :], totals[:, 1, :])
 
 

time: 373 us -> 265 us (0.71)
  waiting for transfers between devices: 280 us -> 174 us
    psum x1 -> x0, waiting for transfers between devices: 172 us -> none  [per_device(): totals = lax.psum(partial_value, 'dom')]
    all_gather x0 -> x1, waiting for transfers between devices: none -> 64.8 us  [gather_and_add(): parts = lax.all_gather(value, axis, axis=0, tiled=False)]
where the time goes in v1:
time: 265 us; the launch traced here: 264 us
  waiting for transfers between devices  174 us (66%)
  starting transfers between devices  38.5 us (15%)
  local copies, waits for them, and re-layouts  14.2 us (5%)
  between operations  14.2 us (5%)
  other arithmetic  11.8 us (4%)
  matrix products  11.7 us (4%)
    all_gather x1, waiting for transfers between devices, per_device(): whole_window = lax.all_gather(stacked, 'band', axis=1, tiled=True)  69.7 us
    all_gather x1, waiting for transfers between devices, gather_and_add(): parts = lax.all_gather(value, axis, axis=0, tiled=False)  64.8 us
    ppermute x5, waiting for transfers between devices, padded(): lax.ppermute(lax.slice_in_dim(block, block.shape[dim] - width, None, axis...  33.6 us
    ppermute x5, starting transfers between devices, padded(): lax.ppermute(lax.slice_in_dim(block, 0, width, axis=dim), axis, backward)  20.8 us
    ppermute x5, starting transfers between devices, padded(): lax.ppermute(lax.slice_in_dim(block, block.shape[dim] - width, None, axis...  17.6 us
    dot_general x1, matrix products, per_device(): lax.dot_general(states_flat, flat_piece, (((1,), (1,)), ((), ())), precis...  11.7 us
    reshape x1, local copies, waits for them, and re-layouts, per_device(): flat_piece = whole_window.reshape(-1, states_flat.shape[1])  9.37 us
    ppermute x5, waiting for transfers between devices, padded(): lax.ppermute(lax.slice_in_dim(block, 0, width, axis=dim), axis, backward)  5.42 us
  transfers between devices with their start and end apart: 12, of which 12 were waited for; matrix products, arithmetic and copies ran while one was open for 1% of the time, Pallas kernels for 0%

profile of v1, /device:TPU:8, one launch (start us, length us, event | category | flops | bytes accessed | tf_op | source)
XLA Modules:
  0.0 264.1 jit_solution(17716834653075428853)
XLA Ops:
  7.2 0.0 copy-start
  7.2 0.0 copy-start.1
  7.2 0.0 all-gather.3.cloned.1.call-start
  7.2 1.0 fusion.338
  8.2 13.1 %collective-permute-start = (f32[4,8,6,128]{3,2,1,0:T(8,128)S(1)}, f32[4,8,6,128]{3,2,1,0:T(8,128)S(1)}, u32[]{:S(2)}, u32[]{:S(2)}) collective-permute-start(f32[4,8,6,128]{3,2,1,0:T(8,128)S(1)} %get-tuple-element.24), channel_id=1, source_target_pairs={{1,0},{2,1},{3,2},{4,3},{5,4},{6,5},{7,6},{8,7},{9,8},{10,9},{11,1... | collective-permute-start | bytes 294920 | tf_op jit(solution)/shard_map/ppermute | solution.py:35
  21.4 1.9 collective-permute-start.1
  23.3 1.1 fusion.339
  24.4 0.8 broadcast_multiply_fusion.1
  25.2 0.9 constant_dynamic-update-slice_fusion.1
  26.1 0.8 collective-permute-done
  26.9 7.5 %collective-permute-done.1 = f32[4,8,6,128]{3,2,1,0:T(8,128)S(1)} collective-permute-done((f32[4,8,6,128]{3,2,1,0:T(8,128)S(1)}, f32[4,8,6,128]{3,2,1,0:T(8,128)S(1)}, u32[]{:S(2)}, u32[]{:S(2)}) %collective-permute-start.1) | collective-permute-done | bytes 98336 | tf_op jit(solution)/shard_map/ppermute | solution.py:32
  34.5 5.2 %broadcast_multiply_fusion = (f32[4,8,8,128]{3,2,1,0:T(8,128)S(1)}, f32[4,8,8,128]{3,2,1,0:T(8,128)S(1)}) fusion(f32[4,8,8,128]{3,2,1,0:T(8,128)} %param.4, f32[8,8,128]{2,1,0:T(8,128)} %param.5, f32[4,8,8,6]{3,2,1,0:T(8,128)S(1)} %get-tuple-element.27, f32[4,8,8,6]{3,2,1,0:T(8,128)S(1)} %get-tuple-element.26, ...), kind=kLoop, calls=%fused_computation.601 | loop fusion | flops 2195456 | bytes 1323008 | tf_op jit(solution)/shard_map/div | solution.py:73
  39.7 1.9 collective-permute-start.2
  41.7 3.9 %collective-permute-start.3 = (f32[4,8,6,128]{3,2,1,0:T(8,128)S(1)}, f32[4,8,6,128]{3,2,1,0:T(8,128)S(1)}, u32[]{:S(2)}, u32[]{:S(2)}) collective-permute-start(f32[4,8,6,128]{3,2,1,0:T(8,128)S(1)} %get-tuple-element.21), channel_id=1, source_target_pairs={{0,1},{1,2},{2,3},{3,4},{4,5},{5,6},{6,7},{7,8},{8,9},{9,10},{10,1... | collective-permute-start | bytes 294920 | tf_op jit(solution)/shard_map/ppermute | solution.py:32
  45.6 0.1 fusion.337
  45.7 1.8 collective-permute-done.2
  47.5 7.0 %collective-permute-done.3 = f32[4,8,6,128]{3,2,1,0:T(8,128)S(1)} collective-permute-done((f32[4,8,6,128]{3,2,1,0:T(8,128)S(1)}, f32[4,8,6,128]{3,2,1,0:T(8,128)S(1)}, u32[]{:S(2)}, u32[]{:S(2)}) %collective-permute-start.3) | collective-permute-done | bytes 98336 | tf_op jit(solution)/shard_map/ppermute | solution.py:32
  54.5 0.0 copy-done
  54.5 0.9 fusion.195
  55.4 1.9 collective-permute-start.4
  57.3 3.9 %collective-permute-start.5 = (f32[4,8,6,128]{3,2,1,0:T(8,128)S(1)}, f32[4,8,6,128]{3,2,1,0:T(8,128)S(1)}, u32[]{:S(2)}, u32[]{:S(2)}) collective-permute-start(f32[4,8,6,128]{3,2,1,0:T(8,128)S(1)} %get-tuple-element.17), channel_id=1, source_target_pairs={{0,1},{1,2},{2,3},{3,4},{4,5},{5,6},{6,7},{7,8},{8,9},{9,10},{10,1... | collective-permute-start | bytes 294920 | tf_op jit(solution)/shard_map/ppermute | solution.py:32
  61.2 0.1 fusion.335
  61.3 0.9 collective-permute-done.4
  62.3 6.2 %collective-permute-done.5 = f32[4,8,6,128]{3,2,1,0:T(8,128)S(1)} collective-permute-done((f32[4,8,6,128]{3,2,1,0:T(8,128)S(1)}, f32[4,8,6,128]{3,2,1,0:T(8,128)S(1)}, u32[]{:S(2)}, u32[]{:S(2)}) %collective-permute-start.5) | collective-permute-done | bytes 98336 | tf_op jit(solution)/shard_map/ppermute | solution.py:32
  68.4 0.0 copy-done.1
  68.4 0.9 fusion.134
  69.3 1.9 collective-permute-start.6
  71.2 3.9 %collective-permute-start.7 = (f32[4,8,6,128]{3,2,1,0:T(8,128)S(1)}, f32[4,8,6,128]{3,2,1,0:T(8,128)S(1)}, u32[]{:S(2)}, u32[]{:S(2)}) collective-permute-start(f32[4,8,6,128]{3,2,1,0:T(8,128)S(1)} %get-tuple-element.13), channel_id=1, source_target_pairs={{0,1},{1,2},{2,3},{3,4},{4,5},{5,6},{6,7},{7,8},{8,9},{9,10},{10,1... | collective-permute-start | bytes 294920 | tf_op jit(solution)/shard_map/ppermute | solution.py:32
  75.2 0.1 fusion.333
  75.3 0.9 collective-permute-done.6
  76.2 6.8 %collective-permute-done.7 = f32[4,8,6,128]{3,2,1,0:T(8,128)S(1)} collective-permute-done((f32[4,8,6,128]{3,2,1,0:T(8,128)S(1)}, f32[4,8,6,128]{3,2,1,0:T(8,128)S(1)}, u32[]{:S(2)}, u32[]{:S(2)}) %collective-permute-start.7) | collective-permute-done | bytes 98336 | tf_op jit(solution)/shard_map/ppermute | solution.py:32
  83.0 0.9 fusion.73
  83.8 1.9 collective-permute-start.8
  85.8 3.9 %collective-permute-start.9 = (f32[4,8,6,128]{3,2,1,0:T(8,128)S(1)}, f32[4,8,6,128]{3,2,1,0:T(8,128)S(1)}, u32[]{:S(2)}, u32[]{:S(2)}) collective-permute-start(f32[4,8,6,128]{3,2,1,0:T(8,128)S(1)} %get-tuple-element.9), channel_id=1, source_target_pairs={{0,1},{1,2},{2,3},{3,4},{4,5},{5,6},{6,7},{7,8},{8,9},{9,10},{10,1... | collective-permute-start | bytes 294920 | tf_op jit(solution)/shard_map/ppermute | solution.py:32
  89.7 0.1 fusion.331
  89.8 0.9 collective-permute-done.8
  90.7 6.1 %collective-permute-done.9 = f32[4,8,6,128]{3,2,1,0:T(8,128)S(1)} collective-permute-done((f32[4,8,6,128]{3,2,1,0:T(8,128)S(1)}, f32[4,8,6,128]{3,2,1,0:T(8,128)S(1)}, u32[]{:S(2)}, u32[]{:S(2)}) %collective-permute-start.9) | collective-permute-done | bytes 98336 | tf_op jit(solution)/shard_map/ppermute | solution.py:32
  96.8 0.9 fusion.12
  97.7 0.8 pad_maximum_fusion
  98.4 0.0 all-gather.3.cloned.1.call-update
  98.5 0.0 all-gather.5.cloned.1.call-start
  98.5 69.7 %all-gather.3.cloned.1.call-done = f32[2,128,8,8,128]{4,3,2,1,0:T(8,128)} async-done(((f32[2,4,8,8,128]{4,3,2,1,0:T(8,128)}), f32[2,128,8,8,128]{4,3,2,1,0:T(8,128)}) %all-gather.3.cloned.1.call-update) | async-done | bytes 8388624 | tf_op jit(solution)/shard_map/all_gather | solution.py:84
  168.2 9.4 %reshape.11 = f32[256,8192]{1,0:T(8,128)} reshape(f32[2,128,8,8,128]{4,3,2,1,0:T(8,128)} %all-gather.3.cloned.1.call-done) | data formatting | bytes 16777216 | tf_op jit(solution)/shard_map/reshape | solution.py:85
  177.6 11.7 %fusion = f32[256,128]{1,0:T(8,128)S(1)} fusion(f32[256,8192]{1,0:T(8,128)} %reshape.11, f32[16,8,64,128]{3,2,1,0:T(8,128)} %bitcast.21), kind=kOutput, calls=%fused_computation | convolution fusion | flops 3221225472 | bytes 12713984 | tf_op jit(solution)/shard_map/dot_general | solution.py:86
  189.3 0.7 copy.5
  190.1 0.0 all-gather.5.cloned.1.call-update
  190.1 64.8 %all-gather.5.cloned.1.call-done = f32[16,128,2,128]{3,1,2,0:T(8,128)} async-done(((f32[1,128,2,128]{3,1,2,0:T(8,128)}), f32[16,128,2,128]{3,1,2,0:T(8,128)}) %all-gather.5.cloned.1.call-update) | async-done | bytes 2097168 | tf_op jit(solution)/shard_map/all_gather | solution.py:21
  254.9 1.7 reduce_sum.9
  256.6 0.7 slice_bitcast_fusion
  (5 shorter events, 0.1 us)
Async XLA Ops:
  7.2 47.3 %copy-start = (f32[4,8,8,128]{3,2,1,0:T(8,128)S(1)}, f32[4,8,8,128]{3,2,1,0:T(8,128)}, u32[]{:S(2)}) copy-start(f32[4,8,8,128]{3,2,1,0:T(8,128)} %param.4) | copy-start | bytes 393220
  7.2 61.2 %copy-start.1 = (f32[8,8,128]{2,1,0:T(8,128)S(1)}, f32[8,8,128]{2,1,0:T(8,128)}, u32[]{:S(2)}) copy-start(f32[8,8,128]{2,1,0:T(8,128)} %param.5) | copy-start | bytes 98308
  7.2 161.1 %all-gather.3.cloned.1.call-start = ((), (), s32[]{:S(2)}) async-start(), calls=%async_computation | async-start | bytes 8650752 | tf_op jit(solution)/shard_map/all_gather | solution.py:84
  8.2 18.7 %collective-permute-start = (f32[4,8,6,128]{3,2,1,0:T(8,128)S(1)}, f32[4,8,6,128]{3,2,1,0:T(8,128)S(1)}, u32[]{:S(2)}, u32[]{:S(2)}) collective-permute-start(f32[4,8,6,128]{3,2,1,0:T(8,128)S(1)} %get-tuple-element.24), channel_id=1, source_target_pairs={{1,0},{2,1},{3,2},{4,3},{5,4},{6,5},{7,6},{8,7},{9,8},{10,9},{11,1... | collective-permute-start | bytes 294920 | tf_op jit(solution)/shard_map/ppermute | solution.py:35
  21.4 13.1 %collective-permute-start.1 = (f32[4,8,6,128]{3,2,1,0:T(8,128)S(1)}, f32[4,8,6,128]{3,2,1,0:T(8,128)S(1)}, u32[]{:S(2)}, u32[]{:S(2)}) collective-permute-start(f32[4,8,6,128]{3,2,1,0:T(8,128)S(1)} %get-tuple-element.25), channel_id=1, source_target_pairs={{0,1},{1,2},{2,3},{3,4},{4,5},{5,6},{6,7},{7,8},{8,9},{9,10},{10,1... | collective-permute-start | bytes 294920 | tf_op jit(solution)/shard_map/ppermute | solution.py:32
  39.7 7.8 %collective-permute-start.2 = (f32[4,8,6,128]{3,2,1,0:T(8,128)S(1)}, f32[4,8,6,128]{3,2,1,0:T(8,128)S(1)}, u32[]{:S(2)}, u32[]{:S(2)}) collective-permute-start(f32[4,8,6,128]{3,2,1,0:T(8,128)S(1)} %get-tuple-element.20), channel_id=1, source_target_pairs={{1,0},{2,1},{3,2},{4,3},{5,4},{6,5},{7,6},{8,7},{9,8},{10,9},{11,1... | collective-permute-start | bytes 294920 | tf_op jit(solution)/shard_map/ppermute | solution.py:35
  41.7 12.8 %collective-permute-start.3 = (f32[4,8,6,128]{3,2,1,0:T(8,128)S(1)}, f32[4,8,6,128]{3,2,1,0:T(8,128)S(1)}, u32[]{:S(2)}, u32[]{:S(2)}) collective-permute-start(f32[4,8,6,128]{3,2,1,0:T(8,128)S(1)} %get-tuple-element.21), channel_id=1, source_target_pairs={{0,1},{1,2},{2,3},{3,4},{4,5},{5,6},{6,7},{7,8},{8,9},{9,10},{10,1... | collective-permute-start | bytes 294920 | tf_op jit(solution)/shard_map/ppermute | solution.py:32
  55.4 6.9 %collective-permute-start.4 = (f32[4,8,6,128]{3,2,1,0:T(8,128)S(1)}, f32[4,8,6,128]{3,2,1,0:T(8,128)S(1)}, u32[]{:S(2)}, u32[]{:S(2)}) collective-permute-start(f32[4,8,6,128]{3,2,1,0:T(8,128)S(1)} %get-tuple-element.16), channel_id=1, source_target_pairs={{1,0},{2,1},{3,2},{4,3},{5,4},{6,5},{7,6},{8,7},{9,8},{10,9},{11,1... | collective-permute-start | bytes 294920 | tf_op jit(solution)/shard_map/ppermute | solution.py:35
  57.3 11.1 %collective-permute-start.5 = (f32[4,8,6,128]{3,2,1,0:T(8,128)S(1)}, f32[4,8,6,128]{3,2,1,0:T(8,128)S(1)}, u32[]{:S(2)}, u32[]{:S(2)}) collective-permute-start(f32[4,8,6,128]{3,2,1,0:T(8,128)S(1)} %get-tuple-element.17), channel_id=1, source_target_pairs={{0,1},{1,2},{2,3},{3,4},{4,5},{5,6},{6,7},{7,8},{8,9},{9,10},{10,1... | collective-permute-start | bytes 294920 | tf_op jit(solution)/shard_map/ppermute | solution.py:32
  69.3 6.9 %collective-permute-start.6 = (f32[4,8,6,128]{3,2,1,0:T(8,128)S(1)}, f32[4,8,6,128]{3,2,1,0:T(8,128)S(1)}, u32[]{:S(2)}, u32[]{:S(2)}) collective-permute-start(f32[4,8,6,128]{3,2,1,0:T(8,128)S(1)} %get-tuple-element.12), channel_id=1, source_target_pairs={{1,0},{2,1},{3,2},{4,3},{5,4},{6,5},{7,6},{8,7},{9,8},{10,9},{11,1... | collective-permute-start | bytes 294920 | tf_op jit(solution)/shard_map/ppermute | solution.py:35
  71.2 11.7 %collective-permute-start.7 = (f32[4,8,6,128]{3,2,1,0:T(8,128)S(1)}, f32[4,8,6,128]{3,2,1,0:T(8,128)S(1)}, u32[]{:S(2)}, u32[]{:S(2)}) collective-permute-start(f32[4,8,6,128]{3,2,1,0:T(8,128)S(1)} %get-tuple-element.13), channel_id=1, source_target_pairs={{0,1},{1,2},{2,3},{3,4},{4,5},{5,6},{6,7},{7,8},{8,9},{9,10},{10,1... | collective-permute-start | bytes 294920 | tf_op jit(solution)/shard_map/ppermute | solution.py:32
  83.8 6.9 %collective-permute-start.8 = (f32[4,8,6,128]{3,2,1,0:T(8,128)S(1)}, f32[4,8,6,128]{3,2,1,0:T(8,128)S(1)}, u32[]{:S(2)}, u32[]{:S(2)}) collective-permute-start(f32[4,8,6,128]{3,2,1,0:T(8,128)S(1)} %get-tuple-element.8), channel_id=1, source_target_pairs={{1,0},{2,1},{3,2},{4,3},{5,4},{6,5},{7,6},{8,7},{9,8},{10,9},{11,1... | collective-permute-start | bytes 294920 | tf_op jit(solution)/shard_map/ppermute | solution.py:35
  85.8 11.1 %collective-permute-start.9 = (f32[4,8,6,128]{3,2,1,0:T(8,128)S(1)}, f32[4,8,6,128]{3,2,1,0:T(8,128)S(1)}, u32[]{:S(2)}, u32[]{:S(2)}) collective-permute-start(f32[4,8,6,128]{3,2,1,0:T(8,128)S(1)} %get-tuple-element.9), channel_id=1, source_target_pairs={{0,1},{1,2},{2,3},{3,4},{4,5},{5,6},{6,7},{7,8},{8,9},{9,10},{10,1... | collective-permute-start | bytes 294920 | tf_op jit(solution)/shard_map/ppermute | solution.py:32
  98.5 156.4 %all-gather.5.cloned.1.call-start = ((), (), s32[]{:S(2)}) async-start(), calls=%async_computation.1 | async-start | bytes 2228224 | tf_op jit(solution)/shard_map/all_gather | solution.py:21
Sparse Core Ops, SparseCore 0:
  98.6 69.6 all-gather.2
  190.2 64.5 all-gather.4
